TPU v7x, 32 devices: a whole 2x2x4 slice. The times are simulated.
32 devices in a mesh: groups: 2 (over x), expert: 16 (over z, y, core).
Axes of the slice: x: 2, y: 2, z: 4, core: 2. Of those that a mesh axis runs over, the one named last changes fastest.
Arguments:
- tokens: bfloat16 [384, 3584], P(('groups', 'expert')), parts along dimension 0, may hold values from -6 to 6
- expert_ids: int32 [384, 8], P(('groups', 'expert')), parts along dimension 0, may hold values from 0 to 15, all different within a row; in each aligned block of 12 rows (0 to 11, 12 to 23, ...) at most 8 rows name the same one
- gate_weights: float32 [384, 8], P(('groups', 'expert')), parts along dimension 0, may hold values from 0.1 to 1
- w_gate: bfloat16 [16, 3584, 2048], P('expert'), may hold values from -0.09375 to 0.09375
- w_up: bfloat16 [16, 3584, 2048], P('expert'), may hold values from -0.09375 to 0.09375
- w_down: bfloat16 [16, 2048, 3584], P('expert'), may hold values from -0.125 to 0.125
Outputs:
- moe_out: bfloat16 [384, 3584], P(('groups', 'expert')), parts along dimension 0
There are 2 independent parts, one for each index of `groups`. A program takes and returns all parts, laid end to end along the dimension named above; an argument that names none is the same for every part. Nothing has to cross between parts.
Inputs may be any that keep to these rules, and one draw needn't show every extreme that they name: `expert_ids`: each row names 8 different experts. Within the rows of one block (one device's 12 tokens) no expert is named more than 8 times, and in every draw some expert is named exactly 8 times in some block.
All inputs are finite; a program needn't handle non-finite values.
Results may differ from a plain program's by a relative error of at most 0.005.
Values may be sent and summed in bfloat16 or wider, within the bound.
A program may use at most 128 MiB of HBM per device.

v0:
```python
import jax
import jax.numpy as jnp
from jax import lax
from jax.sharding import PartitionSpec as P

EXPERTS = 16
CAP = 8


def route_tables(expert_ids, gate_weights):
    is_expert = (expert_ids[:, :, None] == jnp.arange(EXPERTS, dtype=jnp.int32)).astype(jnp.int32)
    counts = jnp.sum(is_expert, axis=1)
    before = jnp.cumsum(counts, axis=0) - counts
    slot_index = jnp.sum(is_expert * before[:, None, :], axis=2)
    at_slot = (slot_index[:, :, None] == jnp.arange(CAP, dtype=jnp.int32)).astype(jnp.float32)
    expert_float = is_expert.astype(jnp.float32)
    pick_table = jnp.einsum("tje,tjc->ect", expert_float, at_slot).astype(jnp.bfloat16)
    weighted = expert_float * gate_weights[:, :, None]
    mixing = jnp.einsum("tje,tjc->tec", weighted, at_slot, precision=lax.Precision.HIGHEST)
    return (pick_table, mixing.reshape(expert_ids.shape[0], EXPERTS * CAP))


def body(tokens, expert_ids, gate_weights, w_gate, w_up, w_down):
    shards = lax.axis_size("expert") // EXPERTS
    width = tokens.shape[1]
    local_rows = tokens.shape[0]
    gate_slice, up_slice, down_slice = (w_gate[0], w_up[0], w_down[0])
    pick_table, mixing = route_tables(expert_ids, gate_weights)
    slot_rows = jnp.dot(
        pick_table.reshape(EXPERTS * CAP, local_rows), tokens, preferred_element_type=jnp.float32
    )
    slot_rows = slot_rows.astype(jnp.bfloat16).reshape(EXPERTS, CAP, width)
    outgoing = jnp.broadcast_to(slot_rows[None], (shards, EXPERTS, CAP, width)).reshape(
        shards * EXPERTS, CAP, width
    )
    items = lax.all_to_all(outgoing, "expert", split_axis=0, concat_axis=0, tiled=True)
    flat_rows = items.reshape(-1, width)
    gate_act = jnp.dot(flat_rows, gate_slice, preferred_element_type=jnp.float32)
    up_act = jnp.dot(flat_rows, up_slice, preferred_element_type=jnp.float32)
    hidden = (jax.nn.silu(gate_act) * up_act).astype(jnp.bfloat16)
    returned_parts = lax.all_to_all(
        jnp.dot(hidden, down_slice, preferred_element_type=jnp.float32).reshape(items.shape),
        "expert",
        split_axis=0,
        concat_axis=0,
        tiled=True,
    )
    summed = jnp.sum(returned_parts.reshape(shards, EXPERTS, CAP, width), axis=0)
    combined = jnp.dot(
        mixing,
        summed.reshape(EXPERTS * CAP, width),
        precision=lax.Precision.HIGHEST,
        preferred_element_type=jnp.float32,
    )
    return combined.astype(jnp.bfloat16)


def solution(mesh):
    return jax.shard_map(
        body,
        mesh=mesh,
        in_specs=(
            P(("groups", "expert"), None),
            P(("groups", "expert"), None),
            P(("groups", "expert"), None),
            P("expert", None, None),
            P("expert", None, None),
            P("expert", None, None),
        ),
        out_specs=P(("groups", "expert"), None),
        check_vma=False,
    )
```

profile of v0, /device:TPU:15, one launch (start us, length us, event | category | flops | bytes accessed | tf_op | source)
XLA Modules:
  0.0 100.7 jit_solution(3877577457363186526)
XLA Ops:
  0.0 0.0 copy-start
  0.0 0.8 copy.12
  0.8 0.1 convert_reduce_fusion
  0.9 0.3 select_reduce_fusion
  1.3 0.2 fusion.19
  1.5 0.1 copy.14
  1.6 0.1 reshape.26
  1.7 0.0 copy-done
  1.7 0.4 fusion.6
  2.2 28.3 %all_to_all.10 = bf16[16,8,3584]{2,1,0:T(8,128)(2,1)S(1)} all-to-all(bf16[16,8,3584]{2,1,0:T(8,128)(2,1)S(1)} %fusion.6), channel_id=1, replica_groups=mesh['groups'=2,'expert'=16] {'expert'}, dimensions={0} | all-to-all | bytes 1835008 | tf_op jit(solution)/shard_map/all_to_all | solution.py:36
  30.5 7.2 %fusion.4 = f32[128,2048]{1,0:T(8,128)S(1)} fusion(bf16[1,3584,2048]{2,1,0:T(8,128)(2,1)} %param.9, bf16[16,8,3584]{2,1,0:T(8,128)(2,1)S(1)} %all_to_all.10), kind=kOutput, calls=%fused_computation.4 | convolution fusion | flops 1879048192 | bytes 16646144 | tf_op jit(solution)/shard_map/dot_general | solution.py:38
  37.7 0.0 copy-start.1
  37.7 14.7 %fusion = f32[16,8,3584]{2,1,0:T(8,128)} fusion(bf16[1,2048,3584]{2,1,0:T(8,128)(2,1)} %param.11, bf16[1,3584,2048]{2,1,0:T(8,128)(2,1)} %param.10, f32[128,2048]{1,0:T(8,128)S(1)} %fusion.4, bf16[16,8,3584]{2,1,0:T(8,128)(2,1)S(1)} %all_to_all.10), kind=kOutput, calls=%fused_computation | convolution fusion | flops 3759669248 | bytes 33161216 | tf_op jit(solution)/shard_map/dot_general | solution.py:42
  52.4 4.9 %all-to-all-start.1 = ((f32[16,8,3584]{2,1,0:T(8,128)}), f32[16,8,3584]{2,1,0:T(8,128)S(1)}, u32[]{:S(2)}, u32[]{:S(2)}) async-start(f32[16,8,3584]{2,1,0:T(8,128)} %fusion), calls=%async_computation.1 | async-start | bytes 3670016 | tf_op jit(solution)/shard_map/all_to_all | solution.py:41
  57.3 0.0 copy-done.1
  57.3 0.1 copy.13
  57.4 0.2 fusion.30
  57.6 0.1 copy.21
  57.7 41.3 %all-to-all-done.1 = f32[16,8,3584]{2,1,0:T(8,128)S(1)} async-done(((f32[16,8,3584]{2,1,0:T(8,128)}), f32[16,8,3584]{2,1,0:T(8,128)S(1)}, u32[]{:S(2)}, u32[]{:S(2)}) %all-to-all-start.1) | async-done | bytes 1835040 | tf_op jit(solution)/shard_map/all_to_all | solution.py:41
  99.1 1.6 %fusion.7 = bf16[12,3584]{1,0:T(8,128)(2,1)} fusion(f32[12,16,8]{0,2,1:T(8,128)S(1)} %copy.21, f32[16,8,3584]{2,1,0:T(8,128)S(1)} %all-to-all-done.1), kind=kOutput, calls=%fused_computation.9 | convolution fusion | flops 66103296 | bytes 1927168 | tf_op jit(solution)/shard_map/dot_general | solution.py:49
  (2 shorter events, 0.0 us)
Async XLA Ops:
  0.0 1.7 %copy-start = (bf16[12,3584]{1,0:T(8,128)(2,1)S(1)}, bf16[12,3584]{1,0:T(8,128)(2,1)}, u32[]{:S(2)}) copy-start(bf16[12,3584]{1,0:T(8,128)(2,1)} %param.6) | copy-start | bytes 258052
  37.7 19.6 %copy-start.1 = (f32[12,8]{0,1:T(8,128)S(1)}, f32[12,8]{0,1:T(8,128)}, u32[]{:S(2)}) copy-start(f32[12,8]{0,1:T(8,128)} %param.8) | copy-start | bytes 1156
  52.4 46.7 %all-to-all-start.1 = ((f32[16,8,3584]{2,1,0:T(8,128)}), f32[16,8,3584]{2,1,0:T(8,128)S(1)}, u32[]{:S(2)}, u32[]{:S(2)}) async-start(f32[16,8,3584]{2,1,0:T(8,128)} %fusion), calls=%async_computation.1 | async-start | bytes 3670016 | tf_op jit(solution)/shard_map/all_to_all | solution.py:41
where the time goes:
time: 101 us
  waiting for transfers between devices  41.3 us (41%)
  blocking collectives  28.3 us (28%)
  matrix products  24.4 us (24%)
  starting transfers between devices  4.91 us (5%)
  local copies, waits for them, and re-layouts  1.24 us (1%)
    all_to_all x1, waiting for transfers between devices, body(): lax.all_to_all(jnp.dot(hidden, down_slice, preferred_element_type=jnp.flo...  41.3 us
    all_to_all x1, blocking collectives, body(): lax.all_to_all(outgoing, 'expert', split_axis=0, concat_axis=0, tiled=True)  28.3 us
    dot_general x1, matrix products, body(): jnp.dot(hidden, down_slice, preferred_element_type=jnp.float32)  14.7 us
    dot_general x1, matrix products, body(): jnp.dot(flat_rows, gate_slice, preferred_element_type=jnp.float32)  7.23 us
    all_to_all x1, starting transfers between devices, body(): lax.all_to_all(jnp.dot(hidden, down_slice, preferred_element_type=jnp.flo...  4.91 us
  transfers between devices with their start and end apart: 1, of which 1 were waited for; matrix products, arithmetic and copies ran while one was open for 0% of the time, Pallas kernels for 0%

commit v1 on v0

v1 whole, which is shorter than its diff:
```python
import functools

import jax
import jax.numpy as jnp
from jax import lax
from jax.experimental import pallas as pl
from jax.experimental.pallas import tpu as pltpu
from jax.sharding import PartitionSpec as P

EXPERTS = 16
CAP = 8
TILE = 16
LANES = 128
UNITS = 256


def kernel(
    n,
    tok_ref,
    ids_ref,
    gw_ref,
    wg_hbm,
    wu_hbm,
    wd_hbm,
    out_ref,
    gathered,
    wg,
    wu,
    wd,
    rows_in,
    hidden,
    tail_out,
    kept,
    sending,
    landed,
    wsem,
    dsem,
    ag_send,
    ag_recv,
    rs_send,
    rs_recv,
):
    rows, width = tok_ref.shape
    pad = TILE - rows
    parts = rows // pad
    sec = width // (parts + 1)
    packed = parts * sec
    units = wg.shape[1]
    slots = n * CAP
    stages = n.bit_length() - 1
    me = lax.axis_index("expert")

    def partner(bit):
        return me + bit - 2 * bit * ((me // bit) % 2)

    def weight_copies(j):
        cols = pl.ds(j * UNITS, UNITS)
        return (
            pltpu.make_async_copy(wg_hbm.at[0, :, cols], wg.at[:, cols], wsem.at[0, j]),
            pltpu.make_async_copy(wu_hbm.at[0, :, cols], wu.at[:, cols], wsem.at[1, j]),
        )

    def down_copy(s):
        cols = pl.ds(s * sec, sec)
        return pltpu.make_async_copy(wd_hbm.at[0, :, cols], wd.at[:, cols], dsem.at[s])

    barrier = pltpu.get_barrier_semaphore()
    for k in range(stages):
        pl.semaphore_signal(barrier, inc=1, device_id={"expert": partner(1 << k)})

    for j in range(units // UNITS):
        for copy in weight_copies(j):
            copy.start()
    for s in [parts] + list(range(parts)):
        down_copy(s).start()

    lane = lax.broadcasted_iota(jnp.int32, (rows, LANES), 1)
    row = lax.broadcasted_iota(jnp.int32, (rows, LANES), 0)
    weight = jnp.zeros((rows, LANES), jnp.float32)
    for j in range(ids_ref.shape[1]):
        weight = weight + jnp.where(
            ids_ref[:, j : j + 1] == lane % EXPERTS, gw_ref[:, j : j + 1], 0.0
        )
    chosen = jnp.where(weight > 0.0, 1.0, 0.0)
    slot = jnp.zeros((rows, LANES), jnp.float32)
    for t in range(rows - 1):
        slot = slot + jnp.where(row > t, chosen[t : t + 1, :], 0.0)
    first = weight.astype(jnp.bfloat16).astype(jnp.float32)
    second = (weight - first).astype(jnp.bfloat16).astype(jnp.float32)
    third = weight - first - second
    kind = lane // EXPERTS
    route = jnp.where(
        kind == 0,
        slot,
        jnp.where(kind == 1, first, jnp.where(kind == 2, second, jnp.where(kind == 3, third, 0.0))),
    )
    gathered[0:TILE, packed:] = jnp.concatenate(
        [route, jnp.zeros((pad, LANES), jnp.float32)], axis=0
    ).astype(jnp.bfloat16)
    mine = tok_ref[...].astype(jnp.float32)
    for s in range(parts):
        gathered[0:TILE, s * sec : (s + 1) * sec] = jnp.concatenate(
            [mine[:, s * sec : (s + 1) * sec], mine[pad * s : pad * (s + 1), packed:]], axis=0
        ).astype(jnp.bfloat16)

    pl.semaphore_wait(barrier, stages)

    def block(i):
        return gathered.at[pl.ds(i * TILE, TILE), :]

    def gather_copy(k, i):
        to = (1 << k) + i
        return pltpu.make_async_remote_copy(
            src_ref=block(i),
            dst_ref=block(to),
            send_sem=ag_send.at[to],
            recv_sem=ag_recv.at[to],
            device_id={"expert": partner(n >> (k + 1))},
            device_id_type=pl.DeviceIdType.MESH,
        )

    for k in range(stages):
        gather_copy(k, 0).start()
    order = sorted(range(1, n), key=lambda i: (i >= n // 2, bin(i).count("1"), i))
    for i in order:
        k0 = i.bit_length() - 1
        gather_copy(k0, i - (1 << k0)).wait_recv()
        for k in range(k0 + 1, stages):
            gather_copy(k, i).start()

    expert = me % EXPERTS
    all_rows = n * TILE
    lanes = lax.broadcasted_iota(jnp.int32, (all_rows, LANES), 1)
    table = gathered[:, packed:].astype(jnp.float32)
    slot_of = jnp.sum(jnp.where(lanes == expert, table, 0.0), axis=1, keepdims=True)
    weight_of = jnp.sum(
        jnp.where((lanes % EXPERTS == expert) & (lanes >= EXPERTS), table, 0.0),
        axis=1,
        keepdims=True,
    )
    r_at = lax.broadcasted_iota(jnp.int32, (all_rows, slots), 0)
    m_at = lax.broadcasted_iota(jnp.int32, (all_rows, slots), 1)
    mixing = jnp.where(
        (r_at // TILE == m_at // CAP) & (slot_of == (m_at % CAP).astype(jnp.float32)),
        weight_of,
        0.0,
    )
    mixing_t = mixing.T
    slot_weight = jnp.sum(mixing_t, axis=1, keepdims=True)
    place = jnp.where(mixing > 0.0, 1.0, 0.0)
    pick = jnp.where(mixing_t > 0.0, 1.0, 0.0)
    spare = r_at % TILE >= rows
    spare_t = lax.broadcasted_iota(jnp.int32, (slots, all_rows), 1) % TILE >= rows
    place_main = place.astype(jnp.bfloat16)
    pick_main = pick.astype(jnp.bfloat16)

    tail = jnp.zeros((slots, sec), jnp.float32)
    for s in range(parts):
        data = gathered[:, s * sec : (s + 1) * sec]
        rows_in[:, s * sec : (s + 1) * sec] = jnp.dot(
            pick_main, data, preferred_element_type=jnp.float32
        ).astype(jnp.bfloat16)
        pick_tail = jnp.where(spare_t, pltpu.roll(pick, rows - pad * s, 1), 0.0)
        tail = tail + jnp.dot(
            pick_tail.astype(jnp.bfloat16), data, preferred_element_type=jnp.float32
        )
    rows_in[:, packed:] = tail.astype(jnp.bfloat16)

    @pl.loop(0, units // UNITS)
    def _(j):
        for copy in weight_copies(j):
            copy.wait()
        cols = pl.ds(pl.multiple_of(j * UNITS, UNITS), UNITS)
        gate = jnp.dot(rows_in[...], wg[:, cols], preferred_element_type=jnp.float32)
        up = jnp.dot(rows_in[...], wu[:, cols], preferred_element_type=jnp.float32)
        hidden[:, cols] = (gate / (1.0 + jnp.exp(-gate)) * up).astype(jnp.bfloat16)

    def down(s):
        down_copy(s).wait()
        result = jnp.dot(
            hidden[...], wd[:, s * sec : (s + 1) * sec], preferred_element_type=jnp.float32
        )
        return (result * slot_weight).astype(jnp.bfloat16)

    def sum_copy(s, t):
        half = all_rows >> (t + 1)
        span = pl.ds(half, half)
        return pltpu.make_async_remote_copy(
            src_ref=sending.at[s, span, :],
            dst_ref=landed.at[s, span, :],
            send_sem=rs_send.at[s, t],
            recv_sem=rs_recv.at[s, t],
            device_id={"expert": partner(1 << t)},
            device_id_type=pl.DeviceIdType.MESH,
        )

    def first_stage(s):
        here = down(s)
        place_tail = jnp.where(spare, pltpu.roll(place, rows - pad * s, 0), 0.0)
        half = all_rows // 2
        total = jnp.dot(place_main, here, preferred_element_type=jnp.float32) + jnp.dot(
            place_tail.astype(jnp.bfloat16), tail_out[...], preferred_element_type=jnp.float32
        )
        sending[s, half:, :] = total[half:].astype(jnp.bfloat16)
        sum_copy(s, 0).start()
        kept[s] = total[:half]

    def later_stage(s, t):
        sum_copy(s, t - 1).wait_recv()
        half = all_rows >> (t + 1)
        total = kept[s, : 2 * half, :] + landed[s, 2 * half : 4 * half, :].astype(jnp.float32)
        sending[s, half : 2 * half, :] = total[half:].astype(jnp.bfloat16)
        sum_copy(s, t).start()
        kept[s, :half, :] = total[:half]

    def last_stage(s):
        sum_copy(s, stages - 1).wait_recv()
        return kept[s, :TILE, :] + landed[s, TILE : 2 * TILE, :].astype(jnp.float32)

    tail_out[...] = down(parts)
    tails = []
    for step in range(parts + stages):
        for s in range(parts):
            t = step - s
            if t == 0:
                first_stage(s)
        for s in range(parts):
            t = step - s
            if 0 < t < stages:
                later_stage(s, t)
            elif t == stages:
                done = last_stage(s)
                out_ref[:, s * sec : (s + 1) * sec] = done[:rows].astype(jnp.bfloat16)
                tails.append(done[rows:])
    out_ref[:, packed:] = jnp.concatenate(tails, axis=0).astype(jnp.bfloat16)

    for k in range(stages):
        for i in range(1 << k):
            gather_copy(k, i).wait_send()
    for s in range(parts):
        for t in range(stages):
            sum_copy(s, t).wait_send()


def body(tokens, expert_ids, gate_weights, w_gate, w_up, w_down):
    n = lax.axis_size("expert")
    rows, width = tokens.shape
    units = w_gate.shape[2]
    pad = TILE - rows
    parts = rows // pad
    sec = width // (parts + 1)
    stages = n.bit_length() - 1
    vmem = pl.BlockSpec(memory_space=pltpu.VMEM)
    hbm = pl.BlockSpec(memory_space=pl.ANY)
    return pl.pallas_call(
        functools.partial(kernel, n),
        out_shape=jax.ShapeDtypeStruct((rows, width), jnp.bfloat16),
        in_specs=[vmem, vmem, vmem, hbm, hbm, hbm],
        out_specs=vmem,
        scratch_shapes=[
            pltpu.VMEM((n * TILE, parts * sec + LANES), jnp.bfloat16),
            pltpu.VMEM((width, units), jnp.bfloat16),
            pltpu.VMEM((width, units), jnp.bfloat16),
            pltpu.VMEM((units, width), jnp.bfloat16),
            pltpu.VMEM((n * CAP, width), jnp.bfloat16),
            pltpu.VMEM((n * CAP, units), jnp.bfloat16),
            pltpu.VMEM((n * CAP, sec), jnp.bfloat16),
            pltpu.VMEM((parts, n * TILE // 2, sec), jnp.float32),
            pltpu.VMEM((parts, n * TILE, sec), jnp.bfloat16),
            pltpu.VMEM((parts, n * TILE, sec), jnp.bfloat16),
            pltpu.SemaphoreType.DMA((2, units // UNITS)),
            pltpu.SemaphoreType.DMA((parts + 1,)),
            pltpu.SemaphoreType.DMA((n,)),
            pltpu.SemaphoreType.DMA((n,)),
            pltpu.SemaphoreType.DMA((parts, stages)),
            pltpu.SemaphoreType.DMA((parts, stages)),
        ],
        compiler_params=pltpu.CompilerParams(
            collective_id=0, has_side_effects=True, vmem_limit_bytes=60 * 1024 * 1024
        ),
    )(tokens, expert_ids, gate_weights, w_gate, w_up, w_down)


def solution(mesh):
    return jax.shard_map(
        body,
        mesh=mesh,
        in_specs=(
            P(("groups", "expert"), None),
            P(("groups", "expert"), None),
            P(("groups", "expert"), None),
            P("expert", None, None),
            P("expert", None, None),
            P("expert", None, None),
        ),
        out_specs=P(("groups", "expert"), None),
        check_vma=False,
    )
```

time: 101 us -> 53.8 us (0.53)
  the two profiles are of different devices: /device:TPU:15 before, /device:TPU:0 now
where the time goes in v1:
time: 53.8 us; the launch traced here: 53.5 us
  Pallas kernels  49.2 us (91%)
  local copies, waits for them, and re-layouts  4.28 us (8%)
    pallas_call x1, Pallas kernels, body(): pl.pallas_call(functools.partial(kernel, n), out_shape=jax.ShapeDtypeStru...  49.2 us
    unnamed x3, local copies, waits for them, and re-layouts  4.28 us

profile of v1, /device:TPU:0, one launch (start us, length us, event | category | flops | bytes accessed | tf_op | source)
XLA Modules:
  0.0 53.5 jit_solution(17358508294798274767)
XLA Ops:
  0.0 1.4 %copy.7.ids_ref = s32[12,8]{1,0:T(8,128)} copy(s32[12,8]{0,1:T(8,128)} %param.7) | data formatting | bytes 768 | tf_op args[1]
  1.4 1.4 %copy.8.gw_ref = f32[12,8]{1,0:T(8,128)} copy(f32[12,8]{0,1:T(8,128)} %param.8) | data formatting | bytes 768 | tf_op args[2]
  2.7 49.2 %shard_map.64 = bf16[12,3584]{1,0:T(8,128)(2,1)} custom-call(bf16[12,3584]{1,0:T(8,128)(2,1)} %tok_ref.1, s32[12,8]{1,0:T(8,128)} %copy.7.ids_ref, f32[12,8]{1,0:T(8,128)} %copy.8.gw_ref, bf16[1,3584,2048]{2,1,0:T(8,128)(2,1)} %wg_hbm.1, bf16[1,3584,2048]{2,1,0:T(8,128)(2,1)} %wu_hbm.1, bf16[1,2048,3584]{2,1,0:T(8,128)(2,1)} %wd_hbm.1), custom_call_target="tpu_custom_call" | custom-call | tf_op jit(solution)/shard_map/pallas_call | solution.py:255
  52.0 1.6 %copy.10 = bf16[12,3584]{1,0:T(8,128)(2,1)} copy(bf16[12,3584]{1,0:T(8,128)(2,1)} %shard_map.64) | data formatting | bytes 172032

commit v2 on v1

v2 whole, which is shorter than its diff:
```python
import functools

import jax
import jax.numpy as jnp
from jax import lax
from jax.experimental import pallas as pl
from jax.experimental.pallas import tpu as pltpu
from jax.sharding import PartitionSpec as P

EXPERTS = 16
CAP = 8
TILE = 16
LANES = 128
UNITS = 256


def column_spans(size):
    large = -(-size // UNITS) // 2 * UNITS
    if large == 0 or large >= size:
        return [(0, size)]
    return [(0, large), (large, size - large)]


def kernel(
    n,
    tok_hbm,
    ids_ref,
    gw_ref,
    wg_hbm,
    wu_hbm,
    wd_hbm,
    out_ref,
    tok_ref,
    gathered,
    wg,
    wu,
    wd,
    rows_in,
    hidden,
    tail_out,
    kept,
    sending,
    landed,
    tsem,
    wsem,
    dsem,
    ag_send,
    ag_recv,
    rs_send,
    rs_recv,
):
    rows, width = tok_ref.shape
    pad = TILE - rows
    parts = rows // pad
    sec = width // (parts + 1)
    packed = parts * sec
    units = wg.shape[1]
    spans = column_spans(sec)
    descending = [n >> (k + 1) for k in range(n.bit_length() - 1)]
    swapped = list(descending)
    if len(swapped) > 2:
        swapped[-2], swapped[-3] = swapped[-3], swapped[-2]
    slots = n * CAP
    stages = n.bit_length() - 1
    chunks = [(s, u) for u in range(len(spans)) for s in range(parts)]
    me = lax.axis_index("expert")

    def partner(bit):
        return me + bit - 2 * bit * ((me // bit) % 2)

    def weight_copies(j):
        cols = pl.ds(j * UNITS, UNITS)
        return (
            pltpu.make_async_copy(wg_hbm.at[0, :, cols], wg.at[:, cols], wsem.at[0, j]),
            pltpu.make_async_copy(wu_hbm.at[0, :, cols], wu.at[:, cols], wsem.at[1, j]),
        )

    def down_copy(s, u):
        cols = pl.ds(s * sec + spans[u][0], spans[u][1])
        return pltpu.make_async_copy(wd_hbm.at[0, :, cols], wd.at[:, cols], dsem.at[s, u])

    token_copy = pltpu.make_async_copy(tok_hbm, tok_ref, tsem)
    token_copy.start()

    barrier = pltpu.get_barrier_semaphore()
    for k in range(stages):
        pl.semaphore_signal(barrier, inc=1, device_id={"expert": partner(1 << k)})

    for j in range(units // UNITS):
        for copy in weight_copies(j):
            copy.start()
    for u in range(len(spans)):
        for s in [parts] + list(range(parts)):
            down_copy(s, u).start()

    lane = lax.broadcasted_iota(jnp.int32, (rows, LANES), 1)
    row = lax.broadcasted_iota(jnp.int32, (rows, LANES), 0)
    expert_t = lax.broadcasted_iota(jnp.int32, (LANES, rows), 0) % EXPERTS
    weight_t = jnp.zeros((LANES, rows), jnp.float32)
    for j in range(ids_ref.shape[0]):
        weight_t = weight_t + jnp.where(
            ids_ref[j : j + 1, :] == expert_t, gw_ref[j : j + 1, :], 0.0
        )
    weight = weight_t.T
    chosen = jnp.where(weight > 0.0, 1.0, 0.0)
    slot = jnp.zeros((rows, LANES), jnp.float32)
    for t in range(rows - 1):
        slot = slot + jnp.where(row > t, chosen[t : t + 1, :], 0.0)
    first = weight.astype(jnp.bfloat16).astype(jnp.float32)
    second = (weight - first).astype(jnp.bfloat16).astype(jnp.float32)
    third = weight - first - second
    kind = lane // EXPERTS
    route = jnp.where(
        kind == 0,
        slot,
        jnp.where(kind == 1, first, jnp.where(kind == 2, second, jnp.where(kind == 3, third, 0.0))),
    )
    gathered[0:TILE, :LANES] = jnp.concatenate(
        [route, jnp.zeros((pad, LANES), jnp.float32)], axis=0
    ).astype(jnp.bfloat16)
    token_copy.wait()
    mine = tok_ref[...].astype(jnp.float32)
    for s in range(parts):
        gathered[0:TILE, LANES + s * sec : LANES + (s + 1) * sec] = jnp.concatenate(
            [mine[:, s * sec : (s + 1) * sec], mine[pad * s : pad * (s + 1), packed:]], axis=0
        ).astype(jnp.bfloat16)

    pl.semaphore_wait(barrier, stages)

    def position(mask):
        return sum(1 << k for k, bit in enumerate(descending) if mask & bit)

    def order_of(s):
        return swapped if s % 3 == 1 else descending

    def gather_copy(s, mask, bit):
        first_col = 0 if s == 0 else LANES + s * sec
        cols = pl.ds(first_col, LANES + (s + 1) * sec - first_col)
        to = position(mask | bit)
        return pltpu.make_async_remote_copy(
            src_ref=gathered.at[pl.ds(position(mask) * TILE, TILE), cols],
            dst_ref=gathered.at[pl.ds(to * TILE, TILE), cols],
            send_sem=ag_send.at[s, to],
            recv_sem=ag_recv.at[s, to],
            device_id={"expert": partner(bit)},
            device_id_type=pl.DeviceIdType.MESH,
        )

    def came_by(s, mask):
        return [bit for bit in order_of(s) if mask & bit][-1]

    for k in range(stages):
        for s in range(parts):
            gather_copy(s, 0, order_of(s)[k]).start()
    arrivals = [(s, mask) for s in range(parts) for mask in range(1, n)]
    arrivals.sort(key=lambda a: (a[1] & 1, bin(a[1]).count("1"), a[0], -a[1]))
    for s, mask in arrivals:
        bit = came_by(s, mask)
        gather_copy(s, mask - bit, bit).wait_recv()
        bits = order_of(s)
        for later in bits[bits.index(bit) + 1 :]:
            gather_copy(s, mask, later).start()

    expert = me % EXPERTS
    all_rows = n * TILE
    lanes = lax.broadcasted_iota(jnp.int32, (all_rows, LANES), 1)
    table = gathered[:, :LANES].astype(jnp.float32)
    slot_of = jnp.sum(jnp.where(lanes == expert, table, 0.0), axis=1, keepdims=True)
    weight_of = jnp.sum(
        jnp.where((lanes % EXPERTS == expert) & (lanes >= EXPERTS), table, 0.0),
        axis=1,
        keepdims=True,
    )
    r_at = lax.broadcasted_iota(jnp.int32, (all_rows, slots), 0)
    m_at = lax.broadcasted_iota(jnp.int32, (all_rows, slots), 1)
    mixing = jnp.where(
        (r_at // TILE == m_at // CAP) & (slot_of == (m_at % CAP).astype(jnp.float32)),
        weight_of,
        0.0,
    )
    mixing_t = mixing.T
    slot_weight = jnp.sum(mixing_t, axis=1, keepdims=True)
    place = jnp.where(mixing > 0.0, 1.0, 0.0)
    pick = jnp.where(mixing_t > 0.0, 1.0, 0.0)
    spare = r_at % TILE >= rows
    spare_t = lax.broadcasted_iota(jnp.int32, (slots, all_rows), 1) % TILE >= rows
    spot = [
        position(sum(bit for j, bit in enumerate(swapped) if i >> j & 1)) for i in range(n)
    ]
    places = {
        0: place,
        1: jnp.concatenate([place[TILE * i : TILE * (i + 1)] for i in spot], axis=0),
    }
    pick_main = pick.astype(jnp.bfloat16)

    tail = jnp.zeros((slots, sec), jnp.float32)
    for s in range(parts):
        data = gathered[:, LANES + s * sec : LANES + (s + 1) * sec]
        rows_in[:, s * sec : (s + 1) * sec] = jnp.dot(
            pick_main, data, preferred_element_type=jnp.float32
        ).astype(jnp.bfloat16)
        pick_tail = jnp.where(spare_t, pltpu.roll(pick, rows - pad * s, 1), 0.0)
        tail = tail + jnp.dot(
            pick_tail.astype(jnp.bfloat16), data, preferred_element_type=jnp.float32
        )
    rows_in[:, packed:] = tail.astype(jnp.bfloat16)

    @pl.loop(0, units // UNITS)
    def _(j):
        for copy in weight_copies(j):
            copy.wait()
        cols = pl.ds(pl.multiple_of(j * UNITS, UNITS), UNITS)
        gate = jnp.dot(rows_in[...], wg[:, cols], preferred_element_type=jnp.float32)
        up = jnp.dot(rows_in[...], wu[:, cols], preferred_element_type=jnp.float32)
        hidden[:, cols] = (gate / (1.0 + jnp.exp(-gate)) * up).astype(jnp.bfloat16)

    def down(s, u):
        down_copy(s, u).wait()
        at, size = spans[u]
        result = jnp.dot(
            hidden[...],
            wd[:, s * sec + at : s * sec + at + size],
            preferred_element_type=jnp.float32,
        )
        return (result * slot_weight).astype(jnp.bfloat16)

    def sum_copy(c, t):
        s, u = chunks[c]
        half = all_rows >> (t + 1)
        cols = pl.ds(spans[u][0], spans[u][1])
        return pltpu.make_async_remote_copy(
            src_ref=sending.at[s, pl.ds(half, half), cols],
            dst_ref=landed.at[s, pl.ds(half, half), cols],
            send_sem=rs_send.at[c, t],
            recv_sem=rs_recv.at[c, t],
            device_id={"expert": partner(order_of(s)[stages - 1 - t])},
            device_id_type=pl.DeviceIdType.MESH,
        )

    def columns(c):
        s, u = chunks[c]
        return s, slice(spans[u][0], spans[u][0] + spans[u][1])

    def first_stage(c):
        s, u = chunks[c]
        _, cols = columns(c)
        if s == 0:
            tail_out[:, cols] = down(parts, u)
        here = down(s, u)
        spot_of = places[1 if s % 3 == 1 else 0]
        place_tail = jnp.where(spare, pltpu.roll(spot_of, rows - pad * s, 0), 0.0)
        half = all_rows // 2
        total = jnp.dot(
            spot_of.astype(jnp.bfloat16), here, preferred_element_type=jnp.float32
        ) + jnp.dot(
            place_tail.astype(jnp.bfloat16), tail_out[:, cols], preferred_element_type=jnp.float32
        )
        sending[s, half:, cols] = total[half:].astype(jnp.bfloat16)
        sum_copy(c, 0).start()
        kept[s, :, cols] = total[:half]

    def later_stage(c, t):
        s, cols = columns(c)
        sum_copy(c, t - 1).wait_recv()
        half = all_rows >> (t + 1)
        upper = kept[s, half : 2 * half, cols] + landed[s, 3 * half : 4 * half, cols].astype(
            jnp.float32
        )
        sending[s, half : 2 * half, cols] = upper.astype(jnp.bfloat16)
        sum_copy(c, t).start()
        kept[s, :half, cols] = kept[s, :half, cols] + landed[
            s, 2 * half : 3 * half, cols
        ].astype(jnp.float32)

    def last_stage(c):
        s, u = chunks[c]
        _, cols = columns(c)
        sum_copy(c, stages - 1).wait_recv()
        done = kept[s, :TILE, cols] + landed[s, TILE : 2 * TILE, cols].astype(jnp.float32)
        at, size = spans[u]
        out_ref[:, s * sec + at : s * sec + at + size] = done[:rows].astype(jnp.bfloat16)
        tails[u].append(done[rows:])
        if s == parts - 1:
            out_ref[:, packed + at : packed + at + size] = jnp.concatenate(
                tails[u], axis=0
            ).astype(jnp.bfloat16)

    tails = [[] for _ in spans]
    first_stage(0)
    for c in range(1, len(chunks)):
        first_stage(c)
        later_stage(c - 1, 1)
    later_stage(len(chunks) - 1, 1)
    for step in range(len(chunks) + stages):
        for c in range(len(chunks)):
            t = step - c + 2
            if 2 <= t < stages:
                later_stage(c, t)
            elif t == stages:
                last_stage(c)

    for s in range(parts):
        for mask in range(1, n):
            bit = came_by(s, mask)
            gather_copy(s, mask - bit, bit).wait_send()
    for c in range(len(chunks)):
        for t in range(stages):
            sum_copy(c, t).wait_send()


def body(tokens, expert_ids, gate_weights, w_gate, w_up, w_down):
    n = lax.axis_size("expert")
    rows, width = tokens.shape
    units = w_gate.shape[2]
    pad = TILE - rows
    parts = rows // pad
    sec = width // (parts + 1)
    stages = n.bit_length() - 1
    spans = len(column_spans(sec))
    vmem = pl.BlockSpec(memory_space=pltpu.VMEM)
    hbm = pl.BlockSpec(memory_space=pl.ANY)
    return pl.pallas_call(
        functools.partial(kernel, n),
        out_shape=jax.ShapeDtypeStruct((rows, width), jnp.bfloat16),
        in_specs=[hbm, vmem, vmem, hbm, hbm, hbm],
        out_specs=vmem,
        scratch_shapes=[
            pltpu.VMEM((rows, width), jnp.bfloat16),
            pltpu.VMEM((n * TILE, parts * sec + LANES), jnp.bfloat16),
            pltpu.VMEM((width, units), jnp.bfloat16),
            pltpu.VMEM((width, units), jnp.bfloat16),
            pltpu.VMEM((units, width), jnp.bfloat16),
            pltpu.VMEM((n * CAP, width), jnp.bfloat16),
            pltpu.VMEM((n * CAP, units), jnp.bfloat16),
            pltpu.VMEM((n * CAP, sec), jnp.bfloat16),
            pltpu.VMEM((parts, n * TILE // 2, sec), jnp.float32),
            pltpu.VMEM((parts, n * TILE, sec), jnp.bfloat16),
            pltpu.VMEM((parts, n * TILE, sec), jnp.bfloat16),
            pltpu.SemaphoreType.DMA,
            pltpu.SemaphoreType.DMA((2, units // UNITS)),
            pltpu.SemaphoreType.DMA((parts + 1, spans)),
            pltpu.SemaphoreType.DMA((parts, n)),
            pltpu.SemaphoreType.DMA((parts, n)),
            pltpu.SemaphoreType.DMA((parts * spans, stages)),
            pltpu.SemaphoreType.DMA((parts * spans, stages)),
        ],
        compiler_params=pltpu.CompilerParams(
            collective_id=0, has_side_effects=True, vmem_limit_bytes=60 * 1024 * 1024
        ),
    )(tokens, expert_ids.T, gate_weights.T, w_gate, w_up, w_down)


def solution(mesh):
    return jax.shard_map(
        body,
        mesh=mesh,
        in_specs=(
            P(("groups", "expert"), None),
            P(("groups", "expert"), None),
            P(("groups", "expert"), None),
            P("expert", None, None),
            P("expert", None, None),
            P("expert", None, None),
        ),
        out_specs=P(("groups", "expert"), None),
        check_vma=False,
    )
```

time: 53.8 us -> 58.2 us (1.082)
  Pallas kernels: 49.2 us -> 56.4 us
  local copies, waits for them, and re-layouts: 4.28 us -> 1.55 us
    pallas_call x1, Pallas kernels: 49.2 us -> 56.4 us  [body(): pl.pallas_call(functools.partial(kernel, n), out_shape=jax.ShapeDtypeStru...]
    unnamed x3 -> x1, local copies, waits for them, and re-layouts: 4.28 us -> 1.55 us
where the time goes in v2:
time: 58.2 us; the launch traced here: 58 us
  Pallas kernels  56.4 us (97%)
  local copies, waits for them, and re-layouts  1.55 us (3%)
    pallas_call x1, Pallas kernels, body(): pl.pallas_call(functools.partial(kernel, n), out_shape=jax.ShapeDtypeStru...  56.4 us
    unnamed x1, local copies, waits for them, and re-layouts  1.55 us

profile of v2, /device:TPU:0, one launch (start us, length us, event | category | flops | bytes accessed | tf_op | source)
XLA Modules:
  0.0 58.0 jit_solution(3480956550588229463)
XLA Ops:
  0.0 56.4 %shard_map.64 = bf16[12,3584]{1,0:T(8,128)(2,1)} custom-call(bf16[12,3584]{1,0:T(8,128)(2,1)} %tok_hbm.1, s32[8,12]{1,0:T(8,128)} %bitcast.2, f32[8,12]{1,0:T(8,128)} %bitcast.3, bf16[1,3584,2048]{2,1,0:T(8,128)(2,1)} %wg_hbm.1, bf16[1,3584,2048]{2,1,0:T(8,128)(2,1)} %wu_hbm.1, bf16[1,2048,3584]{2,1,0:T(8,128)(2,1)} %wd_hbm.1), custom_call_target="tpu_custom_call" | custom-call | tf_op jit(solution)/shard_map/pallas_call | solution.py:322
  56.4 1.6 %copy.8 = bf16[12,3584]{1,0:T(8,128)(2,1)} copy(bf16[12,3584]{1,0:T(8,128)(2,1)} %shard_map.64) | data formatting | bytes 172032

commit v3 on v2

--- a/solution.py
+++ b/solution.py
@@ -115,13 +115,13 @@
         slot,
         jnp.where(kind == 1, first, jnp.where(kind == 2, second, jnp.where(kind == 3, third, 0.0))),
     )
-    gathered[0:TILE, :LANES] = jnp.concatenate(
+    gathered[0][0:TILE, :LANES] = jnp.concatenate(
         [route, jnp.zeros((pad, LANES), jnp.float32)], axis=0
     ).astype(jnp.bfloat16)
     token_copy.wait()
     mine = tok_ref[...].astype(jnp.float32)
     for s in range(parts):
-        gathered[0:TILE, LANES + s * sec : LANES + (s + 1) * sec] = jnp.concatenate(
+        gathered[s][0:TILE, gathered[s].shape[1] - sec :] = jnp.concatenate(
             [mine[:, s * sec : (s + 1) * sec], mine[pad * s : pad * (s + 1), packed:]], axis=0
         ).astype(jnp.bfloat16)
 
@@ -134,12 +134,10 @@
         return swapped if s % 3 == 1 else descending
 
     def gather_copy(s, mask, bit):
-        first_col = 0 if s == 0 else LANES + s * sec
-        cols = pl.ds(first_col, LANES + (s + 1) * sec - first_col)
         to = position(mask | bit)
         return pltpu.make_async_remote_copy(
-            src_ref=gathered.at[pl.ds(position(mask) * TILE, TILE), cols],
-            dst_ref=gathered.at[pl.ds(to * TILE, TILE), cols],
+            src_ref=gathered[s].at[pl.ds(position(mask) * TILE, TILE), :],
+            dst_ref=gathered[s].at[pl.ds(to * TILE, TILE), :],
             send_sem=ag_send.at[s, to],
             recv_sem=ag_recv.at[s, to],
             device_id={"expert": partner(bit)},
@@ -153,7 +151,7 @@
         for s in range(parts):
             gather_copy(s, 0, order_of(s)[k]).start()
     arrivals = [(s, mask) for s in range(parts) for mask in range(1, n)]
-    arrivals.sort(key=lambda a: (a[1] & 1, bin(a[1]).count("1"), a[0], -a[1]))
+    arrivals.sort(key=lambda a: (a[1] & 1, bin(a[1]).count("1"), a[0], a[1] & 2, a[1]))
     for s, mask in arrivals:
         bit = came_by(s, mask)
         gather_copy(s, mask - bit, bit).wait_recv()
@@ -164,7 +162,7 @@
     expert = me % EXPERTS
     all_rows = n * TILE
     lanes = lax.broadcasted_iota(jnp.int32, (all_rows, LANES), 1)
-    table = gathered[:, :LANES].astype(jnp.float32)
+    table = gathered[0][:, :LANES].astype(jnp.float32)
     slot_of = jnp.sum(jnp.where(lanes == expert, table, 0.0), axis=1, keepdims=True)
     weight_of = jnp.sum(
         jnp.where((lanes % EXPERTS == expert) & (lanes >= EXPERTS), table, 0.0),
@@ -195,7 +193,7 @@
 
     tail = jnp.zeros((slots, sec), jnp.float32)
     for s in range(parts):
-        data = gathered[:, LANES + s * sec : LANES + (s + 1) * sec]
+        data = gathered[s][:, gathered[s].shape[1] - sec :]
         rows_in[:, s * sec : (s + 1) * sec] = jnp.dot(
             pick_main, data, preferred_element_type=jnp.float32
         ).astype(jnp.bfloat16)
@@ -227,10 +225,9 @@
     def sum_copy(c, t):
         s, u = chunks[c]
         half = all_rows >> (t + 1)
-        cols = pl.ds(spans[u][0], spans[u][1])
         return pltpu.make_async_remote_copy(
-            src_ref=sending.at[s, pl.ds(half, half), cols],
-            dst_ref=landed.at[s, pl.ds(half, half), cols],
+            src_ref=sending[u].at[s, pl.ds(half, half), :],
+            dst_ref=landed[u].at[s, pl.ds(half, half), :],
             send_sem=rs_send.at[c, t],
             recv_sem=rs_recv.at[c, t],
             device_id={"expert": partner(order_of(s)[stages - 1 - t])},
@@ -255,28 +252,29 @@
         ) + jnp.dot(
             place_tail.astype(jnp.bfloat16), tail_out[:, cols], preferred_element_type=jnp.float32
         )
-        sending[s, half:, cols] = total[half:].astype(jnp.bfloat16)
+        sending[u][s, half:, :] = total[half:].astype(jnp.bfloat16)
         sum_copy(c, 0).start()
         kept[s, :, cols] = total[:half]
 
     def later_stage(c, t):
-        s, cols = columns(c)
+        s, u = chunks[c]
+        _, cols = columns(c)
         sum_copy(c, t - 1).wait_recv()
         half = all_rows >> (t + 1)
-        upper = kept[s, half : 2 * half, cols] + landed[s, 3 * half : 4 * half, cols].astype(
+        upper = kept[s, half : 2 * half, cols] + landed[u][s, 3 * half : 4 * half, :].astype(
             jnp.float32
         )
-        sending[s, half : 2 * half, cols] = upper.astype(jnp.bfloat16)
+        sending[u][s, half : 2 * half, :] = upper.astype(jnp.bfloat16)
         sum_copy(c, t).start()
-        kept[s, :half, cols] = kept[s, :half, cols] + landed[
-            s, 2 * half : 3 * half, cols
+        kept[s, :half, cols] = kept[s, :half, cols] + landed[u][
+            s, 2 * half : 3 * half, :
         ].astype(jnp.float32)
 
     def last_stage(c):
         s, u = chunks[c]
         _, cols = columns(c)
         sum_copy(c, stages - 1).wait_recv()
-        done = kept[s, :TILE, cols] + landed[s, TILE : 2 * TILE, cols].astype(jnp.float32)
+        done = kept[s, :TILE, cols] + landed[u][s, TILE : 2 * TILE, :].astype(jnp.float32)
         at, size = spans[u]
         out_ref[:, s * sec + at : s * sec + at + size] = done[:rows].astype(jnp.bfloat16)
         tails[u].append(done[rows:])
@@ -291,13 +289,12 @@
         first_stage(c)
         later_stage(c - 1, 1)
     later_stage(len(chunks) - 1, 1)
-    for step in range(len(chunks) + stages):
-        for c in range(len(chunks)):
-            t = step - c + 2
-            if 2 <= t < stages:
-                later_stage(c, t)
-            elif t == stages:
-                last_stage(c)
+    events = [(c + 2.5 * (t - 2), c, t) for c in range(len(chunks)) for t in range(2, stages + 1)]
+    for _, c, t in sorted(events):
+        if t < stages:
+            later_stage(c, t)
+        else:
+            last_stage(c)
 
     for s in range(parts):
         for mask in range(1, n):
@@ -316,7 +313,7 @@
     parts = rows // pad
     sec = width // (parts + 1)
     stages = n.bit_length() - 1
-    spans = len(column_spans(sec))
+    spans = column_spans(sec)
     vmem = pl.BlockSpec(memory_space=pltpu.VMEM)
     hbm = pl.BlockSpec(memory_space=pl.ANY)
     return pl.pallas_call(
@@ -326,7 +323,10 @@
         out_specs=vmem,
         scratch_shapes=[
             pltpu.VMEM((rows, width), jnp.bfloat16),
-            pltpu.VMEM((n * TILE, parts * sec + LANES), jnp.bfloat16),
+            [
+                pltpu.VMEM((n * TILE, sec + (LANES if s == 0 else 0)), jnp.bfloat16)
+                for s in range(parts)
+            ],
             pltpu.VMEM((width, units), jnp.bfloat16),
             pltpu.VMEM((width, units), jnp.bfloat16),
             pltpu.VMEM((units, width), jnp.bfloat16),
@@ -334,15 +334,15 @@
             pltpu.VMEM((n * CAP, units), jnp.bfloat16),
             pltpu.VMEM((n * CAP, sec), jnp.bfloat16),
             pltpu.VMEM((parts, n * TILE // 2, sec), jnp.float32),
-            pltpu.VMEM((parts, n * TILE, sec), jnp.bfloat16),
-            pltpu.VMEM((parts, n * TILE, sec), jnp.bfloat16),
+            [pltpu.VMEM((parts, n * TILE, size), jnp.bfloat16) for _, size in spans],
+            [pltpu.VMEM((parts, n * TILE, size), jnp.bfloat16) for _, size in spans],
             pltpu.SemaphoreType.DMA,
             pltpu.SemaphoreType.DMA((2, units // UNITS)),
-            pltpu.SemaphoreType.DMA((parts + 1, spans)),
+            pltpu.SemaphoreType.DMA((parts + 1, len(spans))),
             pltpu.SemaphoreType.DMA((parts, n)),
             pltpu.SemaphoreType.DMA((parts, n)),
-            pltpu.SemaphoreType.DMA((parts * spans, stages)),
-            pltpu.SemaphoreType.DMA((parts * spans, stages)),
+            pltpu.SemaphoreType.DMA((parts * len(spans), stages)),
+            pltpu.SemaphoreType.DMA((parts * len(spans), stages)),
         ],
         compiler_params=pltpu.CompilerParams(
             collective_id=0, has_side_effects=True, vmem_limit_bytes=60 * 1024 * 1024

time: 58.2 us -> 47.9 us (0.82)
  Pallas kernels: 56.4 us -> 46.1 us
    pallas_call x1, Pallas kernels: 56.4 us -> 46.1 us  [body(): pl.pallas_call(functools.partial(kernel, n), out_shape=jax.ShapeDtypeStru...]
where the time goes in v3:
time: 47.9 us; the launch traced here: 47.6 us
  Pallas kernels  46.1 us (96%)
  local copies, waits for them, and re-layouts  1.55 us (3%)
    pallas_call x1, Pallas kernels, body(): pl.pallas_call(functools.partial(kernel, n), out_shape=jax.ShapeDtypeStru...  46.1 us
    unnamed x1, local copies, waits for them, and re-layouts  1.55 us

profile of v3, /device:TPU:0, one launch (start us, length us, event | category | flops | bytes accessed | tf_op | source)
XLA Modules:
  0.0 47.6 jit_solution(7947322316392349129)
XLA Ops:
  0.0 46.1 %shard_map.64 = bf16[12,3584]{1,0:T(8,128)(2,1)} custom-call(bf16[12,3584]{1,0:T(8,128)(2,1)} %tok_hbm.1, s32[8,12]{1,0:T(8,128)} %bitcast.2, f32[8,12]{1,0:T(8,128)} %bitcast.3, bf16[1,3584,2048]{2,1,0:T(8,128)(2,1)} %wg_hbm.1, bf16[1,3584,2048]{2,1,0:T(8,128)(2,1)} %wu_hbm.1, bf16[1,2048,3584]{2,1,0:T(8,128)(2,1)} %wd_hbm.1), custom_call_target="tpu_custom_call" | custom-call | tf_op jit(solution)/shard_map/pallas_call | solution.py:319
  46.1 1.6 %copy.8 = bf16[12,3584]{1,0:T(8,128)(2,1)} copy(bf16[12,3584]{1,0:T(8,128)(2,1)} %shard_map.64) | data formatting | bytes 172032

commit v4 on v3

--- a/solution.py
+++ b/solution.py
@@ -289,7 +289,7 @@
         first_stage(c)
         later_stage(c - 1, 1)
     later_stage(len(chunks) - 1, 1)
-    events = [(c + 2.5 * (t - 2), c, t) for c in range(len(chunks)) for t in range(2, stages + 1)]
+    events = [(c + 3.5 * (t - 2), c, t) for c in range(len(chunks)) for t in range(2, stages + 1)]
     for _, c, t in sorted(events):
         if t < stages:
             later_stage(c, t)

time: 47.9 us -> 46.2 us (0.965)
  Pallas kernels: 46.1 us -> 44.4 us
    pallas_call x1, Pallas kernels: 46.1 us -> 44.4 us  [body(): pl.pallas_call(functools.partial(kernel, n), out_shape=jax.ShapeDtypeStru...]
where the time goes in v4:
time: 46.2 us; the launch traced here: 46 us
  Pallas kernels  44.4 us (96%)
  local copies, waits for them, and re-layouts  1.55 us (3%)
    pallas_call x1, Pallas kernels, body(): pl.pallas_call(functools.partial(kernel, n), out_shape=jax.ShapeDtypeStru...  44.4 us
    unnamed x1, local copies, waits for them, and re-layouts  1.55 us

profile of v4, /device:TPU:0, one launch (start us, length us, event | category | flops | bytes accessed | tf_op | source)
XLA Modules:
  0.0 46.0 jit_solution(9584646903980648906)
XLA Ops:
  0.0 44.4 %shard_map.64 = bf16[12,3584]{1,0:T(8,128)(2,1)} custom-call(bf16[12,3584]{1,0:T(8,128)(2,1)} %tok_hbm.1, s32[8,12]{1,0:T(8,128)} %bitcast.2, f32[8,12]{1,0:T(8,128)} %bitcast.3, bf16[1,3584,2048]{2,1,0:T(8,128)(2,1)} %wg_hbm.1, bf16[1,3584,2048]{2,1,0:T(8,128)(2,1)} %wu_hbm.1, bf16[1,2048,3584]{2,1,0:T(8,128)(2,1)} %wd_hbm.1), custom_call_target="tpu_custom_call" | custom-call | tf_op jit(solution)/shard_map/pallas_call | solution.py:319
  44.5 1.6 %copy.8 = bf16[12,3584]{1,0:T(8,128)(2,1)} copy(bf16[12,3584]{1,0:T(8,128)(2,1)} %shard_map.64) | data formatting | bytes 172032
